TPU v7x, 32 devices: a whole 2x2x4 slice. The times are simulated.
32 devices in a mesh: expert: 16 (over z, y, x), dp: 2 (over core).
Axes of the slice: x: 2, y: 2, z: 4, core: 2. Of those that a mesh axis runs over, the one named last changes fastest.
Arguments:
- pooled: bfloat16 [8192, 256], P(('expert', 'dp')), may hold values from -6 to 6
- routes: int32 [8192, 2], P(('expert', 'dp')), may hold values from 0 to 15, all different within a row; in each aligned block of 256 rows (0 to 255, 256 to 511, ...) at most 48 rows name the same one
- labels: int32 [8192, 2], P(('expert', 'dp')), may hold values from 0 to 1
- in_weight: bfloat16 [16, 4096, 256], P('expert'), may hold values from -0.375 to 0.375
- out_weight: bfloat16 [16, 4096, 256], P('expert'), may hold values from -0.09375 to 0.09375
- gate_weight: bfloat16 [16, 2, 256], replicated, may hold values from -0.375 to 0.375
- tower_weight: float32 [2, 256], replicated, may hold values from -0.375 to 0.375
- tower_bias: float32 [2], replicated, may hold values from -3 to 3
- bag_rows: int32 [16384], P(('expert', 'dp')), may hold values from 0 to 1023
- bag_sample: int32 [16384], P(('expert', 'dp')), may hold values from 0 to 255
- bag_weight: float32 [16384], P(('expert', 'dp')), may hold values from 0.5 to 2
- row_table: float32 [16384, 256], P('expert'), may hold values from -6 to 6
Outputs:
- in_grad: float32 [16, 4096, 256], P('expert', 'dp')
- out_grad: float32 [16, 4096, 256], P('expert', 'dp')
- gate_grad: float32 [16, 2, 256], P('expert')
- tower_grad: float32 [2, 256], replicated
- new_table: float32 [16384, 256], P('expert')
Inputs may be any that keep to these rules, and one draw needn't show every extreme that they name: `routes`: within each device's 256 rows no expert is named more than 48 times, a bound that some block reaches; a row's two experts differ.
All inputs are finite; a program needn't handle non-finite values.
Results may differ from a plain program's by a relative error of at most 0.0041.
Values may be sent and summed in bfloat16 or wider, within the bound.
A program may use at most 128 MiB of HBM per device.

v0:
```python
import jax
import jax.numpy as jnp
from jax import lax
from jax.sharding import PartitionSpec as P

LOSS_SCALE = 32.0
STEP_SIZE = 0.25
HIGH = lax.Precision.HIGHEST


def silu_grad(pre_silu):
    sigma = jax.nn.sigmoid(pre_silu)
    return sigma * (1.0 + pre_silu * (1.0 - sigma))


def route_slots(routes, owner_count, capacity):
    flat_routes = routes.reshape(-1)
    matches = flat_routes[:, None] == jnp.arange(owner_count, dtype=jnp.int32)[None, :]
    ranks = jnp.cumsum(matches.astype(jnp.int32), axis=0) - 1
    slot_of = jnp.sum(jnp.where(matches, ranks, 0), axis=1)
    return flat_routes * capacity + slot_of


def contract_first(left, right):
    return lax.dot_general(
        left, right, (((0,), (0,)), ((), ())), preferred_element_type=jnp.float32
    )


def contract_last(left, right):
    return lax.dot_general(
        left, right, (((1,), (1,)), ((), ())), preferred_element_type=jnp.float32
    )


def on_device(
    pooled,
    routes,
    labels,
    in_weight,
    out_weight,
    gate_weight,
    tower_weight,
    tower_bias,
    bag_rows,
    bag_sample,
    bag_weight,
    row_table,
):
    owner_count = lax.axis_size("expert")
    tok_rows, feature = pooled.shape
    task_count = tower_weight.shape[0]
    hidden_width = in_weight.shape[1]
    capacity = 3 * tok_rows // owner_count
    slot_index = route_slots(routes, owner_count, capacity)
    in_matrix = in_weight[0]
    out_matrix = out_weight[0]
    paired = jnp.repeat(pooled, 2, axis=0)
    outbound = jnp.zeros((owner_count * capacity, feature), jnp.bfloat16).at[slot_index].set(paired)
    outbound = outbound.reshape(owner_count, capacity, feature)
    received = lax.all_to_all(outbound, "expert", split_axis=0, concat_axis=0, tiled=True)
    sources, slot_count, _ = received.shape
    expert_inputs = received.reshape(sources * slot_count, feature)
    pre_silu = contract_last(expert_inputs, in_matrix)
    expert_hidden_act = jax.nn.silu(pre_silu).astype(jnp.bfloat16)
    result = jnp.dot(expert_hidden_act, out_matrix, preferred_element_type=jnp.float32).astype(
        jnp.bfloat16
    )
    returned = lax.all_to_all(
        result.reshape(sources, slot_count, feature),
        "expert",
        split_axis=0,
        concat_axis=0,
        tiled=True,
    )
    returned, received, pre_stack = (
        returned,
        received,
        pre_silu.reshape(sources, slot_count, hidden_width),
    )
    expert_out = (
        returned.reshape(-1, feature)[slot_index].astype(jnp.float32).reshape(tok_rows, 2, feature)
    )
    experts_all = gate_weight.shape[0]
    one_hot = (
        routes[:, :, None] == jnp.arange(experts_all, dtype=jnp.int32)[None, None, :]
    ).astype(jnp.float32)
    gate_flat = gate_weight.reshape(experts_all * task_count, feature)
    all_logits = contract_last(pooled, gate_flat).reshape(tok_rows, experts_all, task_count)
    chosen = jnp.einsum("nke,net->ntk", one_hot, all_logits, precision=HIGH)
    gate_first = jax.nn.sigmoid(chosen[:, :, 0] - chosen[:, :, 1])
    gate_second = 1.0 - gate_first
    mixture = (
        gate_first[:, :, None] * expert_out[:, None, 0, :]
        + gate_second[:, :, None] * expert_out[:, None, 1, :]
    )
    task_logit = jnp.sum(mixture * tower_weight[None], axis=2) + tower_bias[None]
    logit_grad = LOSS_SCALE * (jax.nn.sigmoid(task_logit) - labels.astype(jnp.float32))
    tower_local = jnp.einsum("nt,ntf->tf", logit_grad, mixture, precision=HIGH)
    mixture_grad = logit_grad[:, :, None] * tower_weight[None]
    routed_grad = jnp.stack(
        [
            jnp.sum(gate_first[:, :, None] * mixture_grad, axis=1),
            jnp.sum(gate_second[:, :, None] * mixture_grad, axis=1),
        ],
        axis=1,
    ).astype(jnp.bfloat16)
    gate_dot = jnp.einsum("ntf,nkf->ntk", mixture_grad, expert_out, precision=HIGH)
    first_grad = (gate_dot[:, :, 0] - gate_dot[:, :, 1]) * gate_first * gate_second
    select_grad = jnp.stack([first_grad, -first_grad], axis=2)
    mix_table = jnp.einsum("nke,ntk->net", one_hot, select_grad, precision=HIGH).reshape(
        tok_rows, experts_all * task_count
    )
    gate_local = lax.dot_general(
        mix_table, pooled.astype(jnp.float32), (((0,), (0,)), ((), ())), precision=HIGH
    ).reshape(experts_all, task_count, feature)
    gate_input = jnp.dot(mix_table, gate_flat.astype(jnp.float32), precision=HIGH)
    grad_outbound = (
        jnp.zeros((owner_count * capacity, feature), jnp.bfloat16)
        .at[slot_index]
        .set(routed_grad.reshape(tok_rows * 2, feature))
    )
    grad_received = lax.all_to_all(
        grad_outbound.reshape(owner_count, capacity, feature),
        "expert",
        split_axis=0,
        concat_axis=0,
        tiled=True,
    )
    inputs = received.reshape(-1, feature)
    grad_rows = grad_received.reshape(-1, feature)
    pre_silu = pre_stack.reshape(-1, hidden_width)
    hidden_act = jax.nn.silu(pre_silu).astype(jnp.bfloat16)
    hidden_grad = contract_last(grad_rows, out_matrix)
    pre_grad = (hidden_grad * silu_grad(pre_silu)).astype(jnp.bfloat16)
    input_rows = jnp.dot(pre_grad, in_matrix, preferred_element_type=jnp.float32).astype(
        jnp.bfloat16
    )
    grad_back = lax.all_to_all(
        input_rows.reshape(owner_count, capacity, feature),
        "expert",
        split_axis=0,
        concat_axis=0,
        tiled=True,
    )
    input_grad = (
        grad_back.reshape(-1, feature)[slot_index].astype(jnp.float32).reshape(tok_rows, 2, feature)
    )
    pooled_grad = gate_input + input_grad[:, 0] + input_grad[:, 1]
    per_owner = bag_rows.shape[0] // owner_count
    row_grads = (
        (bag_weight[:, None] * pooled_grad[bag_sample])
        .astype(jnp.bfloat16)
        .reshape(owner_count, per_owner, feature)
    )
    owned_grads, owned_rows = (
        lax.all_to_all(row_grads, "expert", split_axis=0, concat_axis=0, tiled=True),
        lax.all_to_all(
            bag_rows.reshape(owner_count, per_owner),
            "expert",
            split_axis=0,
            concat_axis=0,
            tiled=True,
        ),
    )
    table_size = row_table.shape[0]
    summed = lax.psum_scatter(
        jnp.concatenate(
            [contract_first(pre_grad, inputs), contract_first(hidden_act, grad_rows)], axis=1
        ),
        "dp",
        scatter_dimension=0,
        tiled=True,
    )
    in_grad = summed[:, :feature][None]
    out_grad = summed[:, feature:][None]
    gate_total, tower_grad = lax.psum((gate_local, tower_local), ("expert", "dp"))
    gate_grad = lax.dynamic_slice_in_dim(gate_total, lax.axis_index("expert"), 1, 0)
    matches = (
        owned_rows.reshape(-1)[:, None] == jnp.arange(table_size, dtype=jnp.int32)[None, :]
    ).astype(jnp.bfloat16)
    row_sums = lax.psum(contract_first(matches, owned_grads.reshape(-1, feature)), "dp")
    new_table = row_table - STEP_SIZE * row_sums
    return (in_grad, out_grad, gate_grad, tower_grad, new_table)


def solution(mesh):
    in_specs = (
        P(("expert", "dp"), None),
        P(("expert", "dp"), None),
        P(("expert", "dp"), None),
        P("expert", None, None),
        P("expert", None, None),
        P(),
        P(),
        P(),
        P(("expert", "dp")),
        P(("expert", "dp")),
        P(("expert", "dp")),
        P("expert", None),
    )
    out_specs = (
        P("expert", "dp", None),
        P("expert", "dp", None),
        P("expert", None, None),
        P(),
        P("expert", None),
    )
    return jax.shard_map(
        on_device, mesh=mesh, in_specs=in_specs, out_specs=out_specs, check_vma=False
    )
```

profile of v0, /device:TPU:0, one launch (start us, length us, event | category | flops | bytes accessed | tf_op | source)
XLA Modules:
  0.0 216.7 jit_solution(16531580779659495678)
XLA Ops:
  12.1 3.1 %scatter_custom_fusion = bf16[768,256]{1,0:T(8,128)(2,1)} fusion(s32[512]{0:T(512)S(1)} %bitcast.112, bf16[512,256]{1,0:T(8,128)(2,1)S(1)} %reshape.166, bf16[]{:T(256)} %constant.13.clone.1), kind=kCustom, calls=%fused_computation.51 | custom fusion | bytes 393218 | tf_op jit(solution)/shard_map/scatter | solution.py:59
  15.2 8.3 %all-to-all-start = ((bf16[16,48,256]{2,1,0:T(8,128)(2,1)}), bf16[16,48,256]{2,1,0:T(8,128)(2,1)S(1)}, u32[]{:S(2)}, u32[]{:S(2)}) async-start(bf16[16,48,256]{2,1,0:T(8,128)(2,1)} %bitcast.5), calls=%async_computation | async-start | bytes 786432 | tf_op jit(solution)/shard_map/all_to_all | solution.py:61
  24.8 11.4 %all-to-all-done = bf16[16,48,256]{2,1,0:T(8,128)(2,1)S(1)} async-done(((bf16[16,48,256]{2,1,0:T(8,128)(2,1)}), bf16[16,48,256]{2,1,0:T(8,128)(2,1)S(1)}, u32[]{:S(2)}, u32[]{:S(2)}) %all-to-all-start) | async-done | bytes 393248 | tf_op jit(solution)/shard_map/all_to_all | solution.py:61
  36.1 6.5 %multiply_convert_fusion.1 = (bf16[768,4096]{1,0:T(8,128)(2,1)S(1)}, f32[768,4096]{1,0:T(8,128)}) fusion(bf16[768,256]{1,0:T(8,128)(2,1)S(1)} %bitcast.101, bf16[1,4096,256]{2,1,0:T(8,128)(2,1)S(1)} %copy-done), kind=kOutput, calls=%fused_computation.6 | convolution fusion | flops 1626341376 | bytes 21364736 | tf_op jit(solution)/shard_map/dot_general | solution.py:31
  47.8 3.7 %all-to-all-start.1 = ((bf16[16,48,256]{2,1,0:T(8,128)(2,1)}), bf16[16,48,256]{2,1,0:T(8,128)(2,1)S(1)}, u32[]{:S(2)}, u32[]{:S(2)}) async-start(bf16[16,48,256]{2,1,0:T(8,128)(2,1)} %bitcast.9), calls=%async_computation.1 | async-start | bytes 786432 | tf_op jit(solution)/shard_map/all_to_all | solution.py:69
  54.0 9.5 %all-to-all-done.1 = bf16[16,48,256]{2,1,0:T(8,128)(2,1)S(1)} async-done(((bf16[16,48,256]{2,1,0:T(8,128)(2,1)}), bf16[16,48,256]{2,1,0:T(8,128)(2,1)S(1)}, u32[]{:S(2)}, u32[]{:S(2)}) %all-to-all-start.1) | async-done | bytes 393248 | tf_op jit(solution)/shard_map/all_to_all | solution.py:69
  63.6 3.7 %all-to-all-start.3 = ((s32[16,1,32]{2,1,0:T(1,128)}), s32[16,1,32]{2,1,0:T(1,128)S(1)}, u32[]{:S(2)}, u32[]{:S(2)}) async-start(s32[16,1,32]{2,1,0:T(1,128)} %all_to_all.24), calls=%async_computation.4 | async-start | bytes 16384 | tf_op jit(solution)/shard_map/all_to_all | solution.py:158
  74.9 3.1 %scatter_custom_fusion.1 = bf16[768,256]{1,0:T(8,128)(2,1)} fusion(s32[512]{0:T(512)S(1)} %bitcast.114, bf16[512,256]{1,0:T(8,128)(2,1)S(1)} %reshape.174, bf16[]{:T(256)} %constant.13.clone.1), kind=kCustom, calls=%fused_computation.49 | custom fusion | bytes 393218 | tf_op jit(solution)/shard_map/scatter | solution.py:121
  78.6 6.8 %all-to-all-start.2 = ((bf16[16,48,256]{2,1,0:T(8,128)(2,1)}), bf16[16,48,256]{2,1,0:T(8,128)(2,1)S(1)}, u32[]{:S(2)}, u32[]{:S(2)}) async-start(bf16[16,48,256]{2,1,0:T(8,128)(2,1)} %bitcast.14), calls=%async_computation.2 | async-start | bytes 786432 | tf_op jit(solution)/shard_map/all_to_all | solution.py:123
  90.0 2.7 %fusion.17 = f32[256,2,2]{1,2,0:T(2,128)} fusion(bf16[256,2,256]{2,1,0:T(2,128)(2,1)S(1)} %gather.14, f32[256,2]{1,0:T(8,128)S(1)} %copy.118, f32[2,256]{1,0:T(2,128)} %param.18), kind=kOutput, calls=%fused_computation.27 | convolution fusion | flops 3276800 | bytes 270336 | tf_op jit(solution)/shard_map/ntf,nkf->ntk/dot_general | solution.py:108
  92.6 3.9 %all-to-all-done.2 = bf16[16,48,256]{2,1,0:T(8,128)(2,1)S(1)} async-done(((bf16[16,48,256]{2,1,0:T(8,128)(2,1)}), bf16[16,48,256]{2,1,0:T(8,128)(2,1)S(1)}, u32[]{:S(2)}, u32[]{:S(2)}) %all-to-all-start.2) | async-done | bytes 393248 | tf_op jit(solution)/shard_map/all_to_all | solution.py:123
  96.6 8.8 %multiply_convert_fusion = bf16[768,4096]{1,0:T(8,128)(2,1)S(1)} fusion(f32[768,4096]{1,0:T(8,128)} %get-tuple-element.56, bf16[768,256]{1,0:T(8,128)(2,1)S(1)} %bitcast.103, bf16[1,4096,256]{2,1,0:T(8,128)(2,1)} %param.16), kind=kOutput, calls=%fused_computation.5 | convolution fusion | flops 1638924288 | bytes 21364736 | tf_op jit(solution)/shard_map/dot_general | solution.py:31
  105.3 2.7 %copy-done.3 = bf16[768,4096]{1,0:T(8,128)(2,1)} copy-done((bf16[768,4096]{1,0:T(8,128)(2,1)}, bf16[768,4096]{1,0:T(8,128)(2,1)S(1)}, u32[]{:S(2)}) %copy-start.3) | copy-done | bytes 6291480
  110.5 3.9 %all-to-all-start.4 = ((bf16[16,48,256]{2,1,0:T(8,128)(2,1)}), bf16[16,48,256]{2,1,0:T(8,128)(2,1)S(1)}, u32[]{:S(2)}, u32[]{:S(2)}) async-start(bf16[16,48,256]{2,1,0:T(8,128)(2,1)} %bitcast.107), calls=%async_computation.5 | async-start | bytes 786432 | tf_op jit(solution)/shard_map/all_to_all | solution.py:139
  117.9 7.9 %all-to-all-done.4 = bf16[16,48,256]{2,1,0:T(8,128)(2,1)S(1)} async-done(((bf16[16,48,256]{2,1,0:T(8,128)(2,1)}), bf16[16,48,256]{2,1,0:T(8,128)(2,1)S(1)}, u32[]{:S(2)}, u32[]{:S(2)}) %all-to-all-start.4) | async-done | bytes 393248 | tf_op jit(solution)/shard_map/all_to_all | solution.py:139
  132.2 3.6 %all-to-all-start.5 = ((bf16[16,32,256]{2,1,0:T(8,128)(2,1)}), bf16[16,32,256]{2,1,0:T(8,128)(2,1)S(1)}, u32[]{:S(2)}, u32[]{:S(2)}) async-start(bf16[16,32,256]{2,1,0:T(8,128)(2,1)} %multiply_convert_fusion.2), calls=%async_computation.6 | async-start | bytes 524288 | tf_op jit(solution)/shard_map/all_to_all | solution.py:157
  135.9 6.7 %fusion.52 = f32[4096,256]{0,1:T(8,128)} fusion(bf16[768,4096]{1,0:T(8,128)(2,1)} %copy-done.2, bf16[768,256]{1,0:T(8,128)(2,1)} %bitcast.104), kind=kOutput, calls=%fused_computation.92 | convolution fusion | flops 1610612736 | bytes 10878976 | tf_op jit(solution)/shard_map/dot_general | solution.py:25
  146.6 4.8 %fusion.51 = f32[4096,256]{0,1:T(8,128)S(1)} fusion(bf16[768,4096]{1,0:T(8,128)(2,1)} %copy-done.3, bf16[768,256]{1,0:T(8,128)(2,1)S(1)} %bitcast.102), kind=kOutput, calls=%fused_computation.91 | convolution fusion | flops 1610612736 | bytes 10878976 | tf_op jit(solution)/shard_map/dot_general | solution.py:25
  151.4 3.8 %pad_maximum_fusion = f32[4096,512]{0,1:T(8,128)} fusion(f32[4096,256]{0,1:T(8,128)S(1)} %copy-done.1, f32[4096,256]{0,1:T(8,128)S(1)} %fusion.51), kind=kLoop, calls=%fused_computation.8 | loop fusion | flops 2097152 | bytes 16777216 | tf_op jit(solution)/shard_map/concatenate | solution.py:168
  156.9 39.3 %all-reduce = (f32[16,2,256]{2,0,1:T(8,128)S(1)}, f32[2,256]{1,0:T(2,128)}) all-reduce(f32[16,2,256]{2,0,1:T(8,128)S(1)} %fusion.32, f32[2,256]{1,0:T(2,128)S(1)} %bitcast.116), channel_id=1, replica_groups=mesh['expert'=16,'dp'=2] {'expert','dp'}, use_global_device_ids=true, to_apply=%region_9.10 | all-reduce | flops 8704 | bytes 69632 | tf_op jit(solution)/shard_map/psum | solution.py:177
  196.8 2.6 %multiply_subtract_fusion = f32[1024,256]{1,0:T(8,128)} fusion(f32[1024,256]{1,0:T(8,128)} %param.23, f32[1024,256]{1,0:T(8,128)} %all-reduce.3.cloned.1.call-done), kind=kLoop, calls=%fused_computation.25 | loop fusion | flops 524288 | bytes 3145728 | tf_op jit(solution)/shard_map/sub | solution.py:183
  199.4 4.7 %slice_bitcast_fusion = (f32[1,2048,256]{1,2,0:T(8,128)}, f32[1,2048,256]{1,2,0:T(8,128)}) fusion(f32[2048,512]{0,1:T(8,128)} %reduce-scatter.2.cloned.1.call-done), kind=kLoop, calls=%fused_computation.9 | loop fusion | bytes 8388608 | tf_op jit(solution)/shard_map/broadcast_in_dim | solution.py:176
  204.1 2.9 %copy.129 = f32[1,2048,256]{2,1,0:T(8,128)} copy(f32[1,2048,256]{1,2,0:T(8,128)} %get-tuple-element.46) | data formatting | bytes 4194304
  207.0 2.9 %copy.130 = f32[1,2048,256]{2,1,0:T(8,128)} copy(f32[1,2048,256]{1,2,0:T(8,128)} %get-tuple-element.45) | data formatting | bytes 4194304
  (123 shorter events, 44.9 us)
Async XLA Ops:
  7.2 29.0 %copy-start = (bf16[1,4096,256]{2,1,0:T(8,128)(2,1)S(1)}, bf16[1,4096,256]{2,1,0:T(8,128)(2,1)}, u32[]{:S(2)}) copy-start(bf16[1,4096,256]{2,1,0:T(8,128)(2,1)} %param.15) | copy-start | bytes 6291460
  15.2 21.0 %all-to-all-start = ((bf16[16,48,256]{2,1,0:T(8,128)(2,1)}), bf16[16,48,256]{2,1,0:T(8,128)(2,1)S(1)}, u32[]{:S(2)}, u32[]{:S(2)}) async-start(bf16[16,48,256]{2,1,0:T(8,128)(2,1)} %bitcast.5), calls=%async_computation | async-start | bytes 786432 | tf_op jit(solution)/shard_map/all_to_all | solution.py:61
  36.1 6.5 %copy-start.4 = (bf16[16,48,256]{2,1,0:T(8,128)(2,1)}, bf16[16,48,256]{2,1,0:T(8,128)(2,1)S(1)}, u32[]{:S(2)}) copy-start(bf16[16,48,256]{2,1,0:T(8,128)(2,1)S(1)} %all-to-all-done) | copy-start | bytes 1179652
  36.1 9.1 %copy-start.23 = (bf16[1,4096,256]{2,1,0:T(8,128)(2,1)S(1)}, bf16[1,4096,256]{2,1,0:T(8,128)(2,1)}, u32[]{:S(2)}) copy-start(bf16[1,4096,256]{2,1,0:T(8,128)(2,1)} %param.16) | copy-start | bytes 6291460
  45.2 8.1 %copy-start.19 = (s32[512]{0:T(512)S(1)}, s32[512]{0:T(512)}, u32[]{:S(2)}) copy-start(s32[512]{0:T(512)} %param.20) | copy-start | bytes 6148
  47.8 22.0 %copy-start.18 = (f32[2,256]{1,0:T(2,128)S(1)}, f32[2,256]{1,0:T(2,128)}, u32[]{:S(2)}) copy-start(f32[2,256]{1,0:T(2,128)} %param.18) | copy-start | bytes 6148
  47.8 23.3 %copy-start.21 = (s32[256,2]{0,1:T(2,128)S(1)}, s32[256,2]{0,1:T(2,128)}, u32[]{:S(2)}) copy-start(s32[256,2]{0,1:T(2,128)} %param.14) | copy-start | bytes 6148
  47.8 23.3 %copy-start.22 = (f32[2]{0:T(128)S(1)}, f32[2]{0:T(128)}, u32[]{:S(2)}) copy-start(f32[2]{0:T(128)} %param.19) | copy-start | bytes 28
  47.8 15.8 %all-to-all-start.1 = ((bf16[16,48,256]{2,1,0:T(8,128)(2,1)}), bf16[16,48,256]{2,1,0:T(8,128)(2,1)S(1)}, u32[]{:S(2)}, u32[]{:S(2)}) async-start(bf16[16,48,256]{2,1,0:T(8,128)(2,1)} %bitcast.9), calls=%async_computation.1 | async-start | bytes 786432 | tf_op jit(solution)/shard_map/all_to_all | solution.py:69
  53.0 14.2 %copy-start.13 = (f32[256,2,1]{0,1,2:T(2,128)}, f32[256,2,1]{0,1,2:T(2,128)S(1)}, u32[]{:S(2)}) copy-start(f32[256,2,1]{0,1,2:T(2,128)S(1)} %get-tuple-element.44) | copy-start | bytes 6148
  54.0 15.7 %copy-start.15 = (s32[1024]{0:T(1024)}, s32[1024]{0:T(1024)S(1)}, u32[]{:S(2)}) copy-start(s32[1024]{0:T(1024)S(1)} %pad_clamp_fusion.1) | copy-start | bytes 12292
  63.6 14.4 %all-to-all-start.3 = ((s32[16,1,32]{2,1,0:T(1,128)}), s32[16,1,32]{2,1,0:T(1,128)S(1)}, u32[]{:S(2)}, u32[]{:S(2)}) async-start(s32[16,1,32]{2,1,0:T(1,128)} %all_to_all.24), calls=%async_computation.4 | async-start | bytes 16384 | tf_op jit(solution)/shard_map/all_to_all | solution.py:158
  78.6 18.0 %all-to-all-start.2 = ((bf16[16,48,256]{2,1,0:T(8,128)(2,1)}), bf16[16,48,256]{2,1,0:T(8,128)(2,1)S(1)}, u32[]{:S(2)}, u32[]{:S(2)}) async-start(bf16[16,48,256]{2,1,0:T(8,128)(2,1)} %bitcast.14), calls=%async_computation.2 | async-start | bytes 786432 | tf_op jit(solution)/shard_map/all_to_all | solution.py:123
  96.6 8.8 %copy-start.6 = (bf16[16,48,256]{2,1,0:T(8,128)(2,1)}, bf16[16,48,256]{2,1,0:T(8,128)(2,1)S(1)}, u32[]{:S(2)}) copy-start(bf16[16,48,256]{2,1,0:T(8,128)(2,1)S(1)} %all-to-all-done.2) | copy-start | bytes 1179652
  108.0 7.9 %copy-start.14 = (f32[256,2,1]{0,1,2:T(2,128)S(1)}, f32[256,2,1]{0,1,2:T(2,128)}, u32[]{:S(2)}) copy-start(f32[256,2,1]{0,1,2:T(2,128)} %copy-done.13) | copy-start | bytes 6148
  108.0 17.8 %copy-start.16 = (s32[1024]{0:T(1024)S(1)}, s32[1024]{0:T(1024)}, u32[]{:S(2)}) copy-start(s32[1024]{0:T(1024)} %copy-done.15) | copy-start | bytes 12292
  110.5 17.9 %copy-start.9 = (bf16[16,2,256]{2,1,0:T(2,128)(2,1)S(1)}, bf16[16,2,256]{2,1,0:T(2,128)(2,1)}, u32[]{:S(2)}) copy-start(bf16[16,2,256]{2,1,0:T(2,128)(2,1)} %param.17) | copy-start | bytes 49156
  110.5 19.2 %copy-start.17 = (s32[1024]{0:T(1024)S(1)}, s32[1024]{0:T(1024)}, u32[]{:S(2)}) copy-start(s32[1024]{0:T(1024)} %pad_clamp_fusion) | copy-start | bytes 12292
  110.5 15.3 %all-to-all-start.4 = ((bf16[16,48,256]{2,1,0:T(8,128)(2,1)}), bf16[16,48,256]{2,1,0:T(8,128)(2,1)S(1)}, u32[]{:S(2)}, u32[]{:S(2)}) async-start(bf16[16,48,256]{2,1,0:T(8,128)(2,1)} %bitcast.107), calls=%async_computation.5 | async-start | bytes 786432 | tf_op jit(solution)/shard_map/all_to_all | solution.py:139
  132.2 12.5 %all-to-all-start.5 = ((bf16[16,32,256]{2,1,0:T(8,128)(2,1)}), bf16[16,32,256]{2,1,0:T(8,128)(2,1)S(1)}, u32[]{:S(2)}, u32[]{:S(2)}) async-start(bf16[16,32,256]{2,1,0:T(8,128)(2,1)} %multiply_convert_fusion.2), calls=%async_computation.6 | async-start | bytes 524288 | tf_op jit(solution)/shard_map/all_to_all | solution.py:157
  135.8 8.9 %copy-start.20 = (s32[512]{0:T(512)S(1)}, s32[512]{0:T(512)}, u32[]{:S(2)}) copy-start(s32[512]{0:T(512)} %eq.64) | copy-start | bytes 6148
  135.8 10.7 %copy-start.5 = (bf16[16,48,256]{2,1,0:T(8,128)(2,1)S(1)}, bf16[16,48,256]{2,1,0:T(8,128)(2,1)}, u32[]{:S(2)}) copy-start(bf16[16,48,256]{2,1,0:T(8,128)(2,1)} %copy-done.4) | copy-start | bytes 1179652
  135.8 60.9 %all-reduce.3.cloned.1.call-start = ((), (), s32[]{:S(2)}) async-start(), calls=%async_computation.8 | async-start | bytes 2097152 | tf_op jit(solution)/shard_map/psum | solution.py:182
  146.5 52.9 %reduce-scatter.2.cloned.1.call-start = ((), (), s32[]{:S(2)}) async-start(), calls=%async_computation.7 | async-start | bytes 12582912 | tf_op jit(solution)/shard_map/reduce_scatter | solution.py:167
  (8 other events, 16.0 us)
Sparse Core Ops, SparseCore 0:
  146.6 18.6 all-reduce.2
  167.6 17.4 reduce-scatter.1
where the time goes:
time: 218 us; the launch traced here: 217 us
  matrix products  42.1 us (19%)
  local copies, waits for them, and re-layouts  40.9 us (19%)
  blocking collectives  39.3 us (18%)
  waiting for transfers between devices  34.8 us (16%)
  starting transfers between devices  30.2 us (14%)
  other arithmetic  14.8 us (7%)
  between operations  14.5 us (7%)
    psum x1, blocking collectives, on_device(): lax.psum((gate_local, tower_local), ('expert', 'dp'))  39.3 us
    dot_general x3, matrix products, contract_last(): lax.dot_general(left, right, (((1,), (1,)), ((), ())), preferred_element_...  16.3 us
    unnamed x57, local copies, waits for them, and re-layouts  14.4 us
    dot_general x3, matrix products, contract_first(): lax.dot_general(left, right, (((0,), (0,)), ((), ())), preferred_element_...  13.3 us
    all_to_all x1, waiting for transfers between devices, on_device(): lax.all_to_all(outbound, 'expert', split_axis=0, concat_axis=0, tiled=True)  11.4 us
    all_to_all x1, waiting for transfers between devices, on_device(): lax.all_to_all(result.reshape(sources, slot_count, feature), 'expert', sp...  9.54 us
    all_to_all x1, starting transfers between devices, on_device(): lax.all_to_all(outbound, 'expert', split_axis=0, concat_axis=0, tiled=True)  8.34 us
    all_to_all x1, waiting for transfers between devices, on_device(): lax.all_to_all(input_rows.reshape(owner_count, capacity, feature), 'exper...  7.88 us
  transfers between devices with their start and end apart: 8, of which 5 were waited for; matrix products, arithmetic and copies ran while one was open for 20% of the time, Pallas kernels for 0%

commit v1 on v0

--- a/solution.py
+++ b/solution.py
@@ -174,7 +174,7 @@
     )
     in_grad = summed[:, :feature][None]
     out_grad = summed[:, feature:][None]
-    gate_total, tower_grad = lax.psum((gate_local, tower_local), ("expert", "dp"))
+    gate_total, tower_grad = lax.psum(lax.psum((gate_local, tower_local), "dp"), "expert")
     gate_grad = lax.dynamic_slice_in_dim(gate_total, lax.axis_index("expert"), 1, 0)
     matches = (
         owned_rows.reshape(-1)[:, None] == jnp.arange(table_size, dtype=jnp.int32)[None, :]

time: 218 us -> 258 us (1.18)
  blocking collectives: 39.3 us -> 79.1 us
    psum x1 -> x2, blocking collectives: 39.3 us -> 79.1 us  [the longest x1 75.7 us: on_device(): lax.psum(lax.psum((gate_local, tower_local), 'dp'), 'expert')]
  transfers between devices with their start and end apart: 8 -> 8, of which waited for: 5 -> 5; matrix products, arithmetic and copies ran while one was open for 20% -> 17% of each run, Pallas kernels for 0% -> 0%
where the time goes in v1:
time: 258 us; the launch traced here: 257 us
  blocking collectives  79.1 us (31%)
  matrix products  42.1 us (16%)
  local copies, waits for them, and re-layouts  40.9 us (16%)
  waiting for transfers between devices  34.8 us (13%)
  starting transfers between devices  30.2 us (12%)
  other arithmetic  14.9 us (6%)
  between operations  14.5 us (6%)
    psum x1, blocking collectives, on_device(): lax.psum(lax.psum((gate_local, tower_local), 'dp'), 'expert')  75.7 us
    dot_general x3, matrix products, contract_last(): lax.dot_general(left, right, (((1,), (1,)), ((), ())), preferred_element_...  16.3 us
    unnamed x57, local copies, waits for them, and re-layouts  14.3 us
    dot_general x3, matrix products, contract_first(): lax.dot_general(left, right, (((0,), (0,)), ((), ())), preferred_element_...  13.3 us
    all_to_all x1, waiting for transfers between devices, on_device(): lax.all_to_all(outbound, 'expert', split_axis=0, concat_axis=0, tiled=True)  11.4 us
    all_to_all x1, waiting for transfers between devices, on_device(): lax.all_to_all(result.reshape(sources, slot_count, feature), 'expert', sp...  9.54 us
    all_to_all x1, starting transfers between devices, on_device(): lax.all_to_all(outbound, 'expert', split_axis=0, concat_axis=0, tiled=True)  8.34 us
    all_to_all x1, waiting for transfers between devices, on_device(): lax.all_to_all(input_rows.reshape(owner_count, capacity, feature), 'exper...  7.89 us
  transfers between devices with their start and end apart: 8, of which 5 were waited for; matrix products, arithmetic and copies ran while one was open for 17% of the time, Pallas kernels for 0%

profile of v1, /device:TPU:0, one launch (start us, length us, event | category | flops | bytes accessed | tf_op | source)
XLA Modules:
  0.0 256.5 jit_solution(5008889264816080463)
XLA Ops:
  12.1 3.1 %scatter_custom_fusion = bf16[768,256]{1,0:T(8,128)(2,1)} fusion(s32[512]{0:T(512)S(1)} %bitcast.112, bf16[512,256]{1,0:T(8,128)(2,1)S(1)} %reshape.166, bf16[]{:T(256)} %constant.13.clone.1), kind=kCustom, calls=%fused_computation.51 | custom fusion | bytes 393218 | tf_op jit(solution)/shard_map/scatter | solution.py:59
  15.2 8.3 %all-to-all-start = ((bf16[16,48,256]{2,1,0:T(8,128)(2,1)}), bf16[16,48,256]{2,1,0:T(8,128)(2,1)S(1)}, u32[]{:S(2)}, u32[]{:S(2)}) async-start(bf16[16,48,256]{2,1,0:T(8,128)(2,1)} %bitcast.5), calls=%async_computation | async-start | bytes 786432 | tf_op jit(solution)/shard_map/all_to_all | solution.py:61
  24.8 11.4 %all-to-all-done = bf16[16,48,256]{2,1,0:T(8,128)(2,1)S(1)} async-done(((bf16[16,48,256]{2,1,0:T(8,128)(2,1)}), bf16[16,48,256]{2,1,0:T(8,128)(2,1)S(1)}, u32[]{:S(2)}, u32[]{:S(2)}) %all-to-all-start) | async-done | bytes 393248 | tf_op jit(solution)/shard_map/all_to_all | solution.py:61
  36.1 6.5 %multiply_convert_fusion.1 = (bf16[768,4096]{1,0:T(8,128)(2,1)S(1)}, f32[768,4096]{1,0:T(8,128)}) fusion(bf16[768,256]{1,0:T(8,128)(2,1)S(1)} %bitcast.101, bf16[1,4096,256]{2,1,0:T(8,128)(2,1)S(1)} %copy-done), kind=kOutput, calls=%fused_computation.6 | convolution fusion | flops 1626341376 | bytes 21364736 | tf_op jit(solution)/shard_map/dot_general | solution.py:31
  47.7 3.7 %all-to-all-start.1 = ((bf16[16,48,256]{2,1,0:T(8,128)(2,1)}), bf16[16,48,256]{2,1,0:T(8,128)(2,1)S(1)}, u32[]{:S(2)}, u32[]{:S(2)}) async-start(bf16[16,48,256]{2,1,0:T(8,128)(2,1)} %bitcast.9), calls=%async_computation.1 | async-start | bytes 786432 | tf_op jit(solution)/shard_map/all_to_all | solution.py:69
  54.0 9.5 %all-to-all-done.1 = bf16[16,48,256]{2,1,0:T(8,128)(2,1)S(1)} async-done(((bf16[16,48,256]{2,1,0:T(8,128)(2,1)}), bf16[16,48,256]{2,1,0:T(8,128)(2,1)S(1)}, u32[]{:S(2)}, u32[]{:S(2)}) %all-to-all-start.1) | async-done | bytes 393248 | tf_op jit(solution)/shard_map/all_to_all | solution.py:69
  63.5 3.7 %all-to-all-start.3 = ((s32[16,1,32]{2,1,0:T(1,128)}), s32[16,1,32]{2,1,0:T(1,128)S(1)}, u32[]{:S(2)}, u32[]{:S(2)}) async-start(s32[16,1,32]{2,1,0:T(1,128)} %all_to_all.24), calls=%async_computation.4 | async-start | bytes 16384 | tf_op jit(solution)/shard_map/all_to_all | solution.py:158
  74.9 3.1 %scatter_custom_fusion.1 = bf16[768,256]{1,0:T(8,128)(2,1)} fusion(s32[512]{0:T(512)S(1)} %bitcast.114, bf16[512,256]{1,0:T(8,128)(2,1)S(1)} %reshape.174, bf16[]{:T(256)} %constant.13.clone.1), kind=kCustom, calls=%fused_computation.49 | custom fusion | bytes 393218 | tf_op jit(solution)/shard_map/scatter | solution.py:121
  78.6 6.8 %all-to-all-start.2 = ((bf16[16,48,256]{2,1,0:T(8,128)(2,1)}), bf16[16,48,256]{2,1,0:T(8,128)(2,1)S(1)}, u32[]{:S(2)}, u32[]{:S(2)}) async-start(bf16[16,48,256]{2,1,0:T(8,128)(2,1)} %bitcast.14), calls=%async_computation.2 | async-start | bytes 786432 | tf_op jit(solution)/shard_map/all_to_all | solution.py:123
  92.6 3.9 %all-to-all-done.2 = bf16[16,48,256]{2,1,0:T(8,128)(2,1)S(1)} async-done(((bf16[16,48,256]{2,1,0:T(8,128)(2,1)}), bf16[16,48,256]{2,1,0:T(8,128)(2,1)S(1)}, u32[]{:S(2)}, u32[]{:S(2)}) %all-to-all-start.2) | async-done | bytes 393248 | tf_op jit(solution)/shard_map/all_to_all | solution.py:123
  96.5 8.8 %multiply_convert_fusion = bf16[768,4096]{1,0:T(8,128)(2,1)S(1)} fusion(f32[768,4096]{1,0:T(8,128)} %get-tuple-element.58, bf16[768,256]{1,0:T(8,128)(2,1)S(1)} %bitcast.103, bf16[1,4096,256]{2,1,0:T(8,128)(2,1)} %param.16), kind=kOutput, calls=%fused_computation.5 | convolution fusion | flops 1638924288 | bytes 21364736 | tf_op jit(solution)/shard_map/dot_general | solution.py:31
  105.3 2.6 %copy-done.3 = bf16[768,4096]{1,0:T(8,128)(2,1)} copy-done((bf16[768,4096]{1,0:T(8,128)(2,1)}, bf16[768,4096]{1,0:T(8,128)(2,1)S(1)}, u32[]{:S(2)}) %copy-start.3) | copy-done | bytes 6291480
  110.5 3.9 %all-to-all-start.4 = ((bf16[16,48,256]{2,1,0:T(8,128)(2,1)}), bf16[16,48,256]{2,1,0:T(8,128)(2,1)S(1)}, u32[]{:S(2)}, u32[]{:S(2)}) async-start(bf16[16,48,256]{2,1,0:T(8,128)(2,1)} %bitcast.107), calls=%async_computation.5 | async-start | bytes 786432 | tf_op jit(solution)/shard_map/all_to_all | solution.py:139
  117.9 7.9 %all-to-all-done.4 = bf16[16,48,256]{2,1,0:T(8,128)(2,1)S(1)} async-done(((bf16[16,48,256]{2,1,0:T(8,128)(2,1)}), bf16[16,48,256]{2,1,0:T(8,128)(2,1)S(1)}, u32[]{:S(2)}, u32[]{:S(2)}) %all-to-all-start.4) | async-done | bytes 393248 | tf_op jit(solution)/shard_map/all_to_all | solution.py:139
  132.1 3.6 %all-to-all-start.5 = ((bf16[16,32,256]{2,1,0:T(8,128)(2,1)}), bf16[16,32,256]{2,1,0:T(8,128)(2,1)S(1)}, u32[]{:S(2)}, u32[]{:S(2)}) async-start(bf16[16,32,256]{2,1,0:T(8,128)(2,1)} %multiply_convert_fusion.2), calls=%async_computation.6 | async-start | bytes 524288 | tf_op jit(solution)/shard_map/all_to_all | solution.py:157
  135.9 6.7 %fusion.52 = f32[4096,256]{0,1:T(8,128)} fusion(bf16[768,4096]{1,0:T(8,128)(2,1)} %copy-done.2, bf16[768,256]{1,0:T(8,128)(2,1)} %bitcast.104), kind=kOutput, calls=%fused_computation.92 | convolution fusion | flops 1610612736 | bytes 10878976 | tf_op jit(solution)/shard_map/dot_general | solution.py:25
  146.6 4.8 %fusion.51 = f32[4096,256]{0,1:T(8,128)S(1)} fusion(bf16[768,4096]{1,0:T(8,128)(2,1)} %copy-done.3, bf16[768,256]{1,0:T(8,128)(2,1)S(1)} %bitcast.102), kind=kOutput, calls=%fused_computation.91 | convolution fusion | flops 1610612736 | bytes 10878976 | tf_op jit(solution)/shard_map/dot_general | solution.py:25
  151.4 3.8 %pad_maximum_fusion = f32[4096,512]{0,1:T(8,128)} fusion(f32[4096,256]{0,1:T(8,128)S(1)} %copy-done.1, f32[4096,256]{0,1:T(8,128)S(1)} %fusion.51), kind=kLoop, calls=%fused_computation.8 | loop fusion | flops 2097152 | bytes 16777216 | tf_op jit(solution)/shard_map/concatenate | solution.py:168
  156.8 3.5 %all-reduce.1 = (f32[16,2,256]{2,0,1:T(8,128)S(1)}, f32[2,256]{1,0:T(2,128)S(1)}) all-reduce(f32[16,2,256]{2,0,1:T(8,128)S(1)} %fusion.32, f32[2,256]{1,0:T(2,128)S(1)} %bitcast.116), channel_id=1, replica_groups=mesh['expert'=16,'dp'=2] {'dp'}, use_global_device_ids=true, to_apply=%region_9.10 | all-reduce | flops 8704 | bytes 69632 | tf_op jit(solution)/shard_map/psum | solution.py:177
  160.3 75.7 %all-reduce = (f32[16,2,256]{2,0,1:T(8,128)S(1)}, f32[2,256]{1,0:T(2,128)}) all-reduce(f32[16,2,256]{2,0,1:T(8,128)S(1)} %get-tuple-element.39, f32[2,256]{1,0:T(2,128)S(1)} %get-tuple-element.40), channel_id=1, replica_groups=mesh['expert'=16,'dp'=2] {'expert'}, use_global_device_ids=true, to_apply=%region_10.11 | all-reduce | flops 8704 | bytes 69632 | tf_op jit(solution)/shard_map/psum | solution.py:177
  236.6 2.6 %multiply_subtract_fusion = f32[1024,256]{1,0:T(8,128)} fusion(f32[1024,256]{1,0:T(8,128)} %param.23, f32[1024,256]{1,0:T(8,128)} %all-reduce.4.cloned.1.call-done), kind=kLoop, calls=%fused_computation.25 | loop fusion | flops 524288 | bytes 3145728 | tf_op jit(solution)/shard_map/sub | solution.py:183
  239.2 4.7 %slice_bitcast_fusion = (f32[1,2048,256]{1,2,0:T(8,128)}, f32[1,2048,256]{1,2,0:T(8,128)}) fusion(f32[2048,512]{0,1:T(8,128)} %reduce-scatter.2.cloned.1.call-done), kind=kLoop, calls=%fused_computation.9 | loop fusion | bytes 8388608 | tf_op jit(solution)/shard_map/broadcast_in_dim | solution.py:176
  243.9 2.9 %copy.129 = f32[1,2048,256]{2,1,0:T(8,128)} copy(f32[1,2048,256]{1,2,0:T(8,128)} %get-tuple-element.48) | data formatting | bytes 4194304
  246.8 2.9 %copy.130 = f32[1,2048,256]{2,1,0:T(8,128)} copy(f32[1,2048,256]{1,2,0:T(8,128)} %get-tuple-element.47) | data formatting | bytes 4194304
  (124 shorter events, 47.6 us)
Async XLA Ops:
  7.2 29.0 %copy-start = (bf16[1,4096,256]{2,1,0:T(8,128)(2,1)S(1)}, bf16[1,4096,256]{2,1,0:T(8,128)(2,1)}, u32[]{:S(2)}) copy-start(bf16[1,4096,256]{2,1,0:T(8,128)(2,1)} %param.15) | copy-start | bytes 6291460
  15.2 21.0 %all-to-all-start = ((bf16[16,48,256]{2,1,0:T(8,128)(2,1)}), bf16[16,48,256]{2,1,0:T(8,128)(2,1)S(1)}, u32[]{:S(2)}, u32[]{:S(2)}) async-start(bf16[16,48,256]{2,1,0:T(8,128)(2,1)} %bitcast.5), calls=%async_computation | async-start | bytes 786432 | tf_op jit(solution)/shard_map/all_to_all | solution.py:61
  36.1 6.5 %copy-start.4 = (bf16[16,48,256]{2,1,0:T(8,128)(2,1)}, bf16[16,48,256]{2,1,0:T(8,128)(2,1)S(1)}, u32[]{:S(2)}) copy-start(bf16[16,48,256]{2,1,0:T(8,128)(2,1)S(1)} %all-to-all-done) | copy-start | bytes 1179652
  36.1 9.1 %copy-start.23 = (bf16[1,4096,256]{2,1,0:T(8,128)(2,1)S(1)}, bf16[1,4096,256]{2,1,0:T(8,128)(2,1)}, u32[]{:S(2)}) copy-start(bf16[1,4096,256]{2,1,0:T(8,128)(2,1)} %param.16) | copy-start | bytes 6291460
  45.2 8.1 %copy-start.19 = (s32[512]{0:T(512)S(1)}, s32[512]{0:T(512)}, u32[]{:S(2)}) copy-start(s32[512]{0:T(512)} %param.20) | copy-start | bytes 6148
  47.7 22.0 %copy-start.18 = (f32[2,256]{1,0:T(2,128)S(1)}, f32[2,256]{1,0:T(2,128)}, u32[]{:S(2)}) copy-start(f32[2,256]{1,0:T(2,128)} %param.18) | copy-start | bytes 6148
  47.7 23.3 %copy-start.21 = (s32[256,2]{0,1:T(2,128)S(1)}, s32[256,2]{0,1:T(2,128)}, u32[]{:S(2)}) copy-start(s32[256,2]{0,1:T(2,128)} %param.14) | copy-start | bytes 6148
  47.7 23.3 %copy-start.22 = (f32[2]{0:T(128)S(1)}, f32[2]{0:T(128)}, u32[]{:S(2)}) copy-start(f32[2]{0:T(128)} %param.19) | copy-start | bytes 28
  47.7 15.8 %all-to-all-start.1 = ((bf16[16,48,256]{2,1,0:T(8,128)(2,1)}), bf16[16,48,256]{2,1,0:T(8,128)(2,1)S(1)}, u32[]{:S(2)}, u32[]{:S(2)}) async-start(bf16[16,48,256]{2,1,0:T(8,128)(2,1)} %bitcast.9), calls=%async_computation.1 | async-start | bytes 786432 | tf_op jit(solution)/shard_map/all_to_all | solution.py:69
  53.0 14.2 %copy-start.13 = (f32[256,2,1]{0,1,2:T(2,128)}, f32[256,2,1]{0,1,2:T(2,128)S(1)}, u32[]{:S(2)}) copy-start(f32[256,2,1]{0,1,2:T(2,128)S(1)} %get-tuple-element.46) | copy-start | bytes 6148
  54.0 15.7 %copy-start.15 = (s32[1024]{0:T(1024)}, s32[1024]{0:T(1024)S(1)}, u32[]{:S(2)}) copy-start(s32[1024]{0:T(1024)S(1)} %pad_clamp_fusion.1) | copy-start | bytes 12292
  63.5 14.4 %all-to-all-start.3 = ((s32[16,1,32]{2,1,0:T(1,128)}), s32[16,1,32]{2,1,0:T(1,128)S(1)}, u32[]{:S(2)}, u32[]{:S(2)}) async-start(s32[16,1,32]{2,1,0:T(1,128)} %all_to_all.24), calls=%async_computation.4 | async-start | bytes 16384 | tf_op jit(solution)/shard_map/all_to_all | solution.py:158
  78.6 18.0 %all-to-all-start.2 = ((bf16[16,48,256]{2,1,0:T(8,128)(2,1)}), bf16[16,48,256]{2,1,0:T(8,128)(2,1)S(1)}, u32[]{:S(2)}, u32[]{:S(2)}) async-start(bf16[16,48,256]{2,1,0:T(8,128)(2,1)} %bitcast.14), calls=%async_computation.2 | async-start | bytes 786432 | tf_op jit(solution)/shard_map/all_to_all | solution.py:123
  96.5 8.8 %copy-start.6 = (bf16[16,48,256]{2,1,0:T(8,128)(2,1)}, bf16[16,48,256]{2,1,0:T(8,128)(2,1)S(1)}, u32[]{:S(2)}) copy-start(bf16[16,48,256]{2,1,0:T(8,128)(2,1)S(1)} %all-to-all-done.2) | copy-start | bytes 1179652
  108.0 7.9 %copy-start.14 = (f32[256,2,1]{0,1,2:T(2,128)S(1)}, f32[256,2,1]{0,1,2:T(2,128)}, u32[]{:S(2)}) copy-start(f32[256,2,1]{0,1,2:T(2,128)} %copy-done.13) | copy-start | bytes 6148
  108.0 17.8 %copy-start.16 = (s32[1024]{0:T(1024)S(1)}, s32[1024]{0:T(1024)}, u32[]{:S(2)}) copy-start(s32[1024]{0:T(1024)} %copy-done.15) | copy-start | bytes 12292
  110.5 17.9 %copy-start.9 = (bf16[16,2,256]{2,1,0:T(2,128)(2,1)S(1)}, bf16[16,2,256]{2,1,0:T(2,128)(2,1)}, u32[]{:S(2)}) copy-start(bf16[16,2,256]{2,1,0:T(2,128)(2,1)} %param.17) | copy-start | bytes 49156
  110.5 19.2 %copy-start.17 = (s32[1024]{0:T(1024)S(1)}, s32[1024]{0:T(1024)}, u32[]{:S(2)}) copy-start(s32[1024]{0:T(1024)} %pad_clamp_fusion) | copy-start | bytes 12292
  110.5 15.3 %all-to-all-start.4 = ((bf16[16,48,256]{2,1,0:T(8,128)(2,1)}), bf16[16,48,256]{2,1,0:T(8,128)(2,1)S(1)}, u32[]{:S(2)}, u32[]{:S(2)}) async-start(bf16[16,48,256]{2,1,0:T(8,128)(2,1)} %bitcast.107), calls=%async_computation.5 | async-start | bytes 786432 | tf_op jit(solution)/shard_map/all_to_all | solution.py:139
  132.1 12.5 %all-to-all-start.5 = ((bf16[16,32,256]{2,1,0:T(8,128)(2,1)}), bf16[16,32,256]{2,1,0:T(8,128)(2,1)S(1)}, u32[]{:S(2)}, u32[]{:S(2)}) async-start(bf16[16,32,256]{2,1,0:T(8,128)(2,1)} %multiply_convert_fusion.2), calls=%async_computation.6 | async-start | bytes 524288 | tf_op jit(solution)/shard_map/all_to_all | solution.py:157
  135.8 8.9 %copy-start.20 = (s32[512]{0:T(512)S(1)}, s32[512]{0:T(512)}, u32[]{:S(2)}) copy-start(s32[512]{0:T(512)} %eq.64) | copy-start | bytes 6148
  135.8 10.7 %copy-start.5 = (bf16[16,48,256]{2,1,0:T(8,128)(2,1)S(1)}, bf16[16,48,256]{2,1,0:T(8,128)(2,1)}, u32[]{:S(2)}) copy-start(bf16[16,48,256]{2,1,0:T(8,128)(2,1)} %copy-done.4) | copy-start | bytes 1179652
  135.8 100.8 %all-reduce.4.cloned.1.call-start = ((), (), s32[]{:S(2)}) async-start(), calls=%async_computation.8 | async-start | bytes 2097152 | tf_op jit(solution)/shard_map/psum | solution.py:182
  146.5 92.7 %reduce-scatter.2.cloned.1.call-start = ((), (), s32[]{:S(2)}) async-start(), calls=%async_computation.7 | async-start | bytes 12582912 | tf_op jit(solution)/shard_map/reduce_scatter | solution.py:167
  (8 other events, 16.0 us)
Sparse Core Ops, SparseCore 0:
  146.6 18.6 all-reduce.3
  167.6 17.4 reduce-scatter.1
